TPU v7x, 32 devices: a whole 2x2x4 slice. The times are simulated.
32 devices in a mesh: node: 4 (over z), dom: 8 (over y, x, core).
Axes of the slice: x: 2, y: 2, z: 4, core: 2. Of those that a mesh axis runs over, the one named last changes fastest.
Arguments:
- probes: float32 [32, 16, 16, 128], P(None, 'dom'), may hold values from -24 to 24
- slope: float32 [16, 16, 128], P('dom'), may hold values from 4 to 6
- root: float32 [16, 16, 128], P('dom'), may hold values from 0.3 to 0.7
- damping: float32 [16, 16, 128], P('dom'), may hold values from 0.3 to 1.2
Outputs:
- moments: float32 [2, 2, 32, 16, 16, 128], P(None, None, 'node', 'dom')
- projections: float32 [2, 2, 32, 32], replicated
All inputs are finite; a program needn't handle non-finite values.
Results may differ from a plain program's by a relative error of at most 0.00013.
Values sent between devices are 32-bit elements; how exact they have to be, the bound alone decides.
A program may use at most 64 MiB of HBM per device.

v0:
```python
import math
import jax
import jax.numpy as jnp
from jax import lax
from jax.sharding import PartitionSpec as P

NODE_DEV = 2
SWEEPS = 8
CENTRE = 0.5
RADIUS = 2.0


def grid_step(source, fields, factor_re, factor_im):
    padded = jnp.pad(fields, ((0, 0), (0, 0), (1, 1), (1, 1), (1, 1)))
    total = padded[:, :, 2:, 1:-1, 1:-1] + padded[:, :, :-2, 1:-1, 1:-1]
    total = total + padded[:, :, 1:-1, 2:, 1:-1] + padded[:, :, 1:-1, :-2, 1:-1]
    total = total + padded[:, :, 1:-1, 1:-1, 2:] + padded[:, :, 1:-1, 1:-1, :-2]
    real_part = source + total[:, 0]
    imag_part = total[:, 1]
    return jnp.stack(
        [
            real_part * factor_re - imag_part * factor_im,
            real_part * factor_im + imag_part * factor_re,
        ],
        axis=1,
    )


def inverse_diagonal(shift_real, shift_imaginary, slope, root, damping, guard):
    zr_col = shift_real[:, None, None, None, None]
    zi_col = shift_imaginary[:, None, None, None, None]
    decay = jnp.exp(-zr_col)
    real_d = slope * (zr_col - root) + damping * (decay * jnp.cos(zi_col))
    imag_d = slope * zi_col - damping * (decay * jnp.sin(zi_col))
    scale = 1.0 / (real_d * real_d + imag_d * imag_d + guard)
    return (real_d * scale, -imag_d * scale)


def per_system(fields, weight_re, weight_im):
    a_col = weight_re[:, None, None, None]
    b_col = weight_im[:, None, None, None]
    return jnp.stack(
        [a_col * fields[:, 0] - b_col * fields[:, 1], a_col * fields[:, 1] + b_col * fields[:, 0]]
    )


def body(probes, slope, root, damping):
    vectors = probes.shape[0]
    planes = probes.shape[1]
    groups = lax.axis_size("node")
    total = NODE_DEV * groups
    first = (lax.axis_index("node") * NODE_DEV).astype(jnp.float32)
    dom_size = lax.axis_size("dom")
    count = NODE_DEV * vectors // dom_size
    replicated = jnp.broadcast_to(probes[None], (NODE_DEV,) + probes.shape).reshape(
        (NODE_DEV * vectors,) + probes.shape[1:]
    )
    own = lax.all_to_all(replicated, "dom", split_axis=0, concat_axis=1, tiled=True)
    slope_all, root_all, damping_all = (
        lax.all_gather(slope, "dom", axis=0, tiled=True),
        lax.all_gather(root, "dom", axis=0, tiled=True),
        lax.all_gather(damping, "dom", axis=0, tiled=True),
    )
    system = lax.axis_index("dom") * count + jnp.arange(count)
    position = first + (system // vectors).astype(jnp.float32)
    theta = 2.0 * math.pi * (position + 0.5) / total
    shift_real = CENTRE + RADIUS * jnp.cos(theta)
    shift_imaginary = RADIUS * jnp.sin(theta)
    qre, qim = inverse_diagonal(
        shift_real, shift_imaginary, slope_all[None], root_all[None], damping_all[None], 0.0
    )
    qre = qre[:, 0]
    qim = qim[:, 0]
    fields = jnp.stack([own * qre, own * qim], axis=1)
    for sweep in range(SWEEPS):
        fields = grid_step(own, fields, qre, qim)
    weight_re = RADIUS * jnp.cos(theta) / total
    weight_im = RADIUS * jnp.sin(theta) / total
    shifted_re = weight_re * shift_real - weight_im * shift_imaginary
    shifted_im = weight_re * shift_imaginary + weight_im * shift_real
    terms = jnp.stack(
        [per_system(fields, weight_re, weight_im), per_system(fields, shifted_re, shifted_im)]
    )
    back = lax.all_to_all(terms, "dom", split_axis=3, concat_axis=2, tiled=True)
    local = jnp.sum(back.reshape((2, 2, NODE_DEV, vectors) + probes.shape[1:]), axis=2)
    flat = local.reshape(4 * vectors, -1)
    basis = probes.reshape(vectors, -1)
    partial_value = lax.dot_general(
        flat,
        basis,
        (((1,), (1,)), ((), ())),
        precision=lax.Precision.HIGHEST,
        preferred_element_type=jnp.float32,
    )
    cells = planes * probes.shape[2] * probes.shape[3] * lax.axis_size("dom")
    projections = lax.psum(partial_value.reshape(2, 2, vectors, vectors) / cells, ("node", "dom"))
    summed = lax.psum(local, "node")
    share = vectors // groups
    moments = lax.dynamic_slice_in_dim(summed, lax.axis_index("node") * share, share, 2)
    return (moments, projections)


def solution(mesh):
    in_specs = (
        P(None, "dom", None, None),
        P("dom", None, None),
        P("dom", None, None),
        P("dom", None, None),
    )
    out_specs = (P(None, None, "node", "dom", None, None), P())
    return jax.shard_map(body, mesh=mesh, in_specs=in_specs, out_specs=out_specs, check_vma=False)
```

profile of v0, /device:TPU:0, one launch (start us, length us, event | category | flops | bytes accessed | tf_op | source)
XLA Modules:
  0.0 260.8 jit_solution(6893673430703613702)
XLA Ops:
  7.2 2.2 broadcast_in_dim.2
  9.4 5.2 %all-to-all-start = ((f32[64,2,16,128]{3,2,1,0:T(8,128)}), f32[64,2,16,128]{3,2,1,0:T(8,128)S(1)}, u32[]{:S(2)}, u32[]{:S(2)}) async-start(f32[64,2,16,128]{3,2,1,0:T(8,128)} %bitcast), calls=%async_computation | async-start | bytes 2097152 | tf_op jit(solution)/shard_map/all_to_all | solution.py:58
  14.6 18.8 %all_gather.9 = f32[16,16,128]{2,1,0:T(8,128)S(1)} all-gather(f32[2,16,128]{2,1,0:T(8,128)S(1)} %copy-done.2), channel_id=1, replica_groups=mesh['node'=4,'dom'=8] {'dom'}, dimensions={0}, use_global_device_ids=true | all-gather | bytes 147456 | tf_op jit(solution)/shard_map/all_gather | solution.py:60
  33.4 8.3 %all_gather.10 = f32[16,16,128]{2,1,0:T(8,128)S(1)} all-gather(f32[2,16,128]{2,1,0:T(8,128)S(1)} %copy-done.3), channel_id=1, replica_groups=mesh['node'=4,'dom'=8] {'dom'}, dimensions={0}, use_global_device_ids=true | all-gather | bytes 147456 | tf_op jit(solution)/shard_map/all_gather | solution.py:61
  41.7 9.1 %all_gather.11 = f32[16,16,128]{2,1,0:T(8,128)S(1)} all-gather(f32[2,16,128]{2,1,0:T(8,128)S(1)} %copy-done.4), channel_id=1, replica_groups=mesh['node'=4,'dom'=8] {'dom'}, dimensions={0}, use_global_device_ids=true | all-gather | bytes 147456 | tf_op jit(solution)/shard_map/all_gather | solution.py:62
  50.8 0.1 multiply_subtract_fusion.12
  50.9 0.0 all-to-all-done
  50.9 0.1 copy.15
  51.0 0.6 fusion.19
  51.6 2.6 select_maximum_fusion.7
  54.2 3.3 %slice_add_fusion.35 = f32[8,2,16,16,128]{4,3,2,0,1:T(8,128)S(1)} fusion(f32[8,2,18,18,130]{4,3,2,0,1:T(8,128)S(1)} %select_maximum_fusion.7), kind=kLoop, calls=%fused_computation.56 | loop fusion | flops 2621440 | bytes 14680064 | tf_op jit(solution)/shard_map/add | solution.py:17
  57.5 0.8 multiply_subtract_fusion.10
  58.3 2.4 select_maximum_fusion.6
  60.7 3.3 %slice_add_fusion.30 = f32[8,2,16,16,128]{4,3,2,0,1:T(8,128)S(1)} fusion(f32[8,2,18,18,130]{4,3,2,0,1:T(8,128)S(1)} %select_maximum_fusion.6), kind=kLoop, calls=%fused_computation.51 | loop fusion | flops 2621440 | bytes 14680064 | tf_op jit(solution)/shard_map/add | solution.py:17
  63.9 0.8 multiply_subtract_fusion.9
  64.7 2.4 select_maximum_fusion.5
  67.1 3.3 %slice_add_fusion.25 = f32[8,2,16,16,128]{4,3,2,0,1:T(8,128)S(1)} fusion(f32[8,2,18,18,130]{4,3,2,0,1:T(8,128)S(1)} %select_maximum_fusion.5), kind=kLoop, calls=%fused_computation.46 | loop fusion | flops 2621440 | bytes 14680064 | tf_op jit(solution)/shard_map/add | solution.py:17
  70.4 0.8 multiply_subtract_fusion.8
  71.2 2.4 select_maximum_fusion.4
  73.6 3.3 %slice_add_fusion.20 = f32[8,2,16,16,128]{4,3,2,0,1:T(8,128)S(1)} fusion(f32[8,2,18,18,130]{4,3,2,0,1:T(8,128)S(1)} %select_maximum_fusion.4), kind=kLoop, calls=%fused_computation.41 | loop fusion | flops 2621440 | bytes 14680064 | tf_op jit(solution)/shard_map/add | solution.py:17
  76.8 0.8 multiply_subtract_fusion.7
  77.6 2.6 select_maximum_fusion.3
  80.2 3.3 %slice_add_fusion.15 = f32[8,2,16,16,128]{4,3,2,0,1:T(8,128)S(1)} fusion(f32[8,2,18,18,130]{4,3,2,0,1:T(8,128)S(1)} %select_maximum_fusion.3), kind=kLoop, calls=%fused_computation.36 | loop fusion | flops 2621440 | bytes 14680064 | tf_op jit(solution)/shard_map/add | solution.py:17
  83.5 0.8 multiply_subtract_fusion.6
  84.3 2.4 select_maximum_fusion.2
  86.7 3.3 %slice_add_fusion.10 = f32[8,2,16,16,128]{4,3,2,0,1:T(8,128)S(1)} fusion(f32[8,2,18,18,130]{4,3,2,0,1:T(8,128)S(1)} %select_maximum_fusion.2), kind=kLoop, calls=%fused_computation.31 | loop fusion | flops 2621440 | bytes 14680064 | tf_op jit(solution)/shard_map/add | solution.py:17
  90.0 0.8 multiply_subtract_fusion.5
  90.8 2.4 select_maximum_fusion.1
  93.1 3.3 %slice_add_fusion.5 = f32[8,2,16,16,128]{4,3,2,0,1:T(8,128)S(1)} fusion(f32[8,2,18,18,130]{4,3,2,0,1:T(8,128)S(1)} %select_maximum_fusion.1), kind=kLoop, calls=%fused_computation.26 | loop fusion | flops 2621440 | bytes 14680064 | tf_op jit(solution)/shard_map/add | solution.py:17
  96.4 0.8 multiply_subtract_fusion.4
  97.2 2.4 select_maximum_fusion
  99.6 3.5 %slice_add_fusion = f32[8,2,16,16,128]{4,3,2,0,1:T(8,128)S(1)} fusion(f32[8,2,18,18,130]{4,3,2,0,1:T(8,128)S(1)} %select_maximum_fusion), kind=kLoop, calls=%fused_computation.21 | loop fusion | flops 2621440 | bytes 14680064 | tf_op jit(solution)/shard_map/add | solution.py:17
  103.1 0.9 multiply_subtract_fusion.1
  104.1 0.5 multiply_subtract_fusion
  104.6 0.4 maximum_bitcast_fusion
  105.0 0.4 pad_maximum_fusion
  105.4 0.6 copy.17
  106.0 51.6 %all_to_all.36 = f32[2,2,8,16,16,128]{5,4,2,1,0,3:T(8,128)S(1)} all-to-all(f32[2,2,8,16,16,128]{5,4,2,1,0,3:T(8,128)S(1)} %copy.17), channel_id=1, replica_groups=mesh['node'=4,'dom'=8] {'dom'}, dimensions={3} | all-to-all | bytes 8388608 | tf_op jit(solution)/shard_map/all_to_all | solution.py:84
  157.6 0.5 copy.19
  158.2 0.0 copy-start.1
  158.2 0.5 bitcast_reduce_fusion
  158.7 0.5 copy-done.1
  159.2 3.1 %fusion.10 = f32[2,2,32,32]{3,2,1,0:T(8,128)S(1)} fusion(f32[2,2,32,2,16,128]{5,4,3,2,1,0:T(8,128)S(1)} %bitcast_reduce_fusion, f32[32,2,16,128,1,1]{3,2,1,0,5,4:T(8,128)S(1)} %bitcast.53), kind=kOutput, calls=%fused_computation.66 | convolution fusion | flops 201330688 | bytes 2637824 | tf_op jit(solution)/shard_map/dot_general | solution.py:88
  162.3 0.0 all-reduce.10.cloned.1.call-start
  162.4 0.7 all-reduce.10.cloned.1.call-update
  163.1 42.9 %psum.15 = f32[2,2,32,32]{3,2,1,0:T(8,128)} all-reduce(f32[2,2,32,32]{3,2,1,0:T(8,128)S(1)} %fusion.10), channel_id=1, replica_groups=mesh['node'=4,'dom'=8] {'node','dom'}, use_global_device_ids=true, to_apply=%region_2.3 | all-reduce | flops 4096 | bytes 32768 | tf_op jit(solution)/shard_map/psum | solution.py:96
  206.0 46.1 %all-reduce.10.cloned.1.call-done = f32[2,2,32,2,16,128]{5,4,3,2,1,0:T(8,128)} async-done(((f32[2,2,32,2,16,128]{5,4,3,2,1,0:T(8,128)}), f32[2,2,32,2,16,128]{5,4,3,2,1,0:T(8,128)}) %all-reduce.10.cloned.1.call-update) | async-done | bytes 2097168 | tf_op jit(solution)/shard_map/psum | solution.py:97
  252.1 1.9 constant_dynamic-slice_fusion
  (9 shorter events, 0.1 us)
Async XLA Ops:
  7.2 7.4 %copy-start.2 = (f32[2,16,128]{2,1,0:T(8,128)S(1)}, f32[2,16,128]{2,1,0:T(8,128)}, u32[]{:S(2)}) copy-start(f32[2,16,128]{2,1,0:T(8,128)} %param.5) | copy-start | bytes 49156
  7.2 26.2 %copy-start.3 = (f32[2,16,128]{2,1,0:T(8,128)S(1)}, f32[2,16,128]{2,1,0:T(8,128)}, u32[]{:S(2)}) copy-start(f32[2,16,128]{2,1,0:T(8,128)} %param.6) | copy-start | bytes 49156
  7.2 34.5 %copy-start.4 = (f32[2,16,128]{2,1,0:T(8,128)S(1)}, f32[2,16,128]{2,1,0:T(8,128)}, u32[]{:S(2)}) copy-start(f32[2,16,128]{2,1,0:T(8,128)} %param.7) | copy-start | bytes 49156
  9.4 41.5 %all-to-all-start = ((f32[64,2,16,128]{3,2,1,0:T(8,128)}), f32[64,2,16,128]{3,2,1,0:T(8,128)S(1)}, u32[]{:S(2)}, u32[]{:S(2)}) async-start(f32[64,2,16,128]{3,2,1,0:T(8,128)} %bitcast), calls=%async_computation | async-start | bytes 2097152 | tf_op jit(solution)/shard_map/all_to_all | solution.py:58
  158.2 1.0 copy-start.1
  158.7 3.6 %copy-start = (f32[2,2,32,2,16,128]{5,4,3,2,1,0:T(8,128)}, f32[2,2,32,2,16,128]{5,4,3,2,1,0:T(8,128)S(1)}, u32[]{:S(2)}) copy-start(f32[2,2,32,2,16,128]{5,4,3,2,1,0:T(8,128)S(1)} %bitcast_reduce_fusion) | copy-start | bytes 6291460
  162.3 89.8 %all-reduce.10.cloned.1.call-start = ((), (), s32[]{:S(2)}) async-start(), calls=%async_computation.2 | async-start | bytes 4194304 | tf_op jit(solution)/shard_map/psum | solution.py:97
Sparse Core Ops, SparseCore 0:
  165.5 86.5 all-reduce.9
where the time goes:
time: 261 us
  blocking collectives  131 us (50%)
  other arithmetic  54.8 us (21%)
  waiting for transfers between devices  46.8 us (18%)
  between operations  14.3 us (5%)
  local copies, waits for them, and re-layouts  5.8 us (2%)
  starting transfers between devices  5.24 us (2%)
  matrix products  3.08 us (1%)
    all_to_all x1, blocking collectives, body(): back = lax.all_to_all(terms, 'dom', split_axis=3, concat_axis=2, tiled=True)  51.6 us
    psum x1, waiting for transfers between devices, body(): summed = lax.psum(local, 'node')  46.1 us
    psum x1, blocking collectives, body(): lax.psum(partial_value.reshape(2, 2, vectors, vectors) / cells, ('node',...  42.9 us
    add x8, other arithmetic, grid_step(): total = total + padded[:, :, 1:-1, 1:-1, 2:] + padded[:, :, 1:-1, 1:-1, :-2]  26.4 us
    all_gather x1, blocking collectives, body(): lax.all_gather(slope, 'dom', axis=0, tiled=True)  18.8 us
    another operation x7, other arithmetic, grid_step(): jnp.stack([real_part * factor_re - imag_part * factor_im, real_part * fac...  16.9 us
    all_gather x1, blocking collectives, body(): lax.all_gather(damping, 'dom', axis=0, tiled=True)  9.1 us
    all_gather x1, blocking collectives, body(): lax.all_gather(root, 'dom', axis=0, tiled=True)  8.31 us
  transfers between devices with their start and end apart: 2, of which 1 were waited for; matrix products, arithmetic and copies ran while one was open for 0% of the time, Pallas kernels for 0%

commit v1 on v0

--- a/solution.py
+++ b/solution.py
@@ -93,7 +93,9 @@
         preferred_element_type=jnp.float32,
     )
     cells = planes * probes.shape[2] * probes.shape[3] * lax.axis_size("dom")
-    projections = lax.psum(partial_value.reshape(2, 2, vectors, vectors) / cells, ("node", "dom"))
+    projections = lax.psum(
+        lax.psum(partial_value.reshape(2, 2, vectors, vectors) / cells, "dom"), "node"
+    )
     summed = lax.psum(local, "node")
     share = vectors // groups
     moments = lax.dynamic_slice_in_dim(summed, lax.axis_index("node") * share, share, 2)

time: 261 us -> 263 us (level)
  blocking collectives: 131 us -> 135 us
  waiting for transfers between devices: 46.8 us -> 43.8 us
    psum x1 -> x2, blocking collectives: 42.9 us -> 46.9 us  [the longest x1 23.5 us: body(): lax.psum(partial_value.reshape(2, 2, vectors, vectors) / cells, 'dom')]
    psum x1, waiting for transfers between devices: 46.1 us -> 43.2 us  [body(): summed = lax.psum(local, 'node')]
where the time goes in v1:
time: 263 us; the launch traced here: 262 us
  blocking collectives  135 us (51%)
  other arithmetic  55.1 us (21%)
  waiting for transfers between devices  43.8 us (17%)
  between operations  14.4 us (5%)
  local copies, waits for them, and re-layouts  5.76 us (2%)
  starting transfers between devices  5.24 us (2%)
  matrix products  3.08 us (1%)
    all_to_all x1, blocking collectives, body(): back = lax.all_to_all(terms, 'dom', split_axis=3, concat_axis=2, tiled=True)  51.6 us
    psum x1, waiting for transfers between devices, body(): summed = lax.psum(local, 'node')  43.2 us
    add x8, other arithmetic, grid_step(): total = total + padded[:, :, 1:-1, 1:-1, 2:] + padded[:, :, 1:-1, 1:-1, :-2]  26.4 us
    psum x1, blocking collectives, body(): lax.psum(partial_value.reshape(2, 2, vectors, vectors) / cells, 'dom')  23.5 us
    psum x1, blocking collectives, body(): lax.psum(lax.psum(partial_value.reshape(2, 2, vectors, vectors) / cells,...  23.4 us
    all_gather x1, blocking collectives, body(): lax.all_gather(slope, 'dom', axis=0, tiled=True)  18.8 us
    another operation x7, other arithmetic, grid_step(): jnp.stack([real_part * factor_re - imag_part * factor_im, real_part * fac...  17.1 us
    all_gather x1, blocking collectives, body(): lax.all_gather(damping, 'dom', axis=0, tiled=True)  9.1 us
  transfers between devices with their start and end apart: 2, of which 1 were waited for; matrix products, arithmetic and copies ran while one was open for 0% of the time, Pallas kernels for 0%

profile of v1, /device:TPU:0, one launch (start us, length us, event | category | flops | bytes accessed | tf_op | source)
XLA Modules:
  0.0 262.1 jit_solution(14924875201755681358)
XLA Ops:
  7.2 2.2 broadcast_in_dim.2
  9.4 5.2 %all-to-all-start = ((f32[64,2,16,128]{3,2,1,0:T(8,128)}), f32[64,2,16,128]{3,2,1,0:T(8,128)S(1)}, u32[]{:S(2)}, u32[]{:S(2)}) async-start(f32[64,2,16,128]{3,2,1,0:T(8,128)} %bitcast), calls=%async_computation | async-start | bytes 2097152 | tf_op jit(solution)/shard_map/all_to_all | solution.py:58
  14.6 18.8 %all_gather.9 = f32[16,16,128]{2,1,0:T(8,128)S(1)} all-gather(f32[2,16,128]{2,1,0:T(8,128)S(1)} %copy-done.2), channel_id=1, replica_groups=mesh['node'=4,'dom'=8] {'dom'}, dimensions={0}, use_global_device_ids=true | all-gather | bytes 147456 | tf_op jit(solution)/shard_map/all_gather | solution.py:60
  33.4 8.3 %all_gather.10 = f32[16,16,128]{2,1,0:T(8,128)S(1)} all-gather(f32[2,16,128]{2,1,0:T(8,128)S(1)} %copy-done.3), channel_id=1, replica_groups=mesh['node'=4,'dom'=8] {'dom'}, dimensions={0}, use_global_device_ids=true | all-gather | bytes 147456 | tf_op jit(solution)/shard_map/all_gather | solution.py:61
  41.7 9.1 %all_gather.11 = f32[16,16,128]{2,1,0:T(8,128)S(1)} all-gather(f32[2,16,128]{2,1,0:T(8,128)S(1)} %copy-done.4), channel_id=1, replica_groups=mesh['node'=4,'dom'=8] {'dom'}, dimensions={0}, use_global_device_ids=true | all-gather | bytes 147456 | tf_op jit(solution)/shard_map/all_gather | solution.py:62
  50.8 0.1 multiply_subtract_fusion.12
  50.9 0.1 copy.15
  51.0 0.6 fusion.19
  51.6 2.6 select_maximum_fusion.7
  54.2 3.3 %slice_add_fusion.35 = f32[8,2,16,16,128]{4,3,2,0,1:T(8,128)S(1)} fusion(f32[8,2,18,18,130]{4,3,2,0,1:T(8,128)S(1)} %select_maximum_fusion.7), kind=kLoop, calls=%fused_computation.56 | loop fusion | flops 2621440 | bytes 14680064 | tf_op jit(solution)/shard_map/add | solution.py:17
  57.5 0.8 multiply_subtract_fusion.10
  58.3 2.4 select_maximum_fusion.6
  60.7 3.3 %slice_add_fusion.30 = f32[8,2,16,16,128]{4,3,2,0,1:T(8,128)S(1)} fusion(f32[8,2,18,18,130]{4,3,2,0,1:T(8,128)S(1)} %select_maximum_fusion.6), kind=kLoop, calls=%fused_computation.51 | loop fusion | flops 2621440 | bytes 14680064 | tf_op jit(solution)/shard_map/add | solution.py:17
  64.0 0.8 multiply_subtract_fusion.9
  64.8 2.4 select_maximum_fusion.5
  67.2 3.3 %slice_add_fusion.25 = f32[8,2,16,16,128]{4,3,2,0,1:T(8,128)S(1)} fusion(f32[8,2,18,18,130]{4,3,2,0,1:T(8,128)S(1)} %select_maximum_fusion.5), kind=kLoop, calls=%fused_computation.46 | loop fusion | flops 2621440 | bytes 14680064 | tf_op jit(solution)/shard_map/add | solution.py:17
  70.5 0.8 multiply_subtract_fusion.8
  71.3 2.4 select_maximum_fusion.4
  73.7 3.3 %slice_add_fusion.20 = f32[8,2,16,16,128]{4,3,2,0,1:T(8,128)S(1)} fusion(f32[8,2,18,18,130]{4,3,2,0,1:T(8,128)S(1)} %select_maximum_fusion.4), kind=kLoop, calls=%fused_computation.41 | loop fusion | flops 2621440 | bytes 14680064 | tf_op jit(solution)/shard_map/add | solution.py:17
  77.0 0.8 multiply_subtract_fusion.7
  77.8 2.6 %select_maximum_fusion.3 = f32[8,2,18,18,130]{4,3,2,0,1:T(8,128)S(1)} fusion(f32[8,1,16,16,128]{4,3,2,0,1:T(8,128)S(1)} %get-tuple-element.17, f32[8,1,16,16,128]{4,3,2,0,1:T(8,128)S(1)} %get-tuple-element.16), kind=kLoop, calls=%fused_computation.9 | loop fusion | flops 12130560 | bytes 4792832 | tf_op jit(solution)/shard_map/stack | solution.py:20
  80.4 3.3 %slice_add_fusion.15 = f32[8,2,16,16,128]{4,3,2,0,1:T(8,128)S(1)} fusion(f32[8,2,18,18,130]{4,3,2,0,1:T(8,128)S(1)} %select_maximum_fusion.3), kind=kLoop, calls=%fused_computation.36 | loop fusion | flops 2621440 | bytes 14680064 | tf_op jit(solution)/shard_map/add | solution.py:17
  83.7 0.8 multiply_subtract_fusion.6
  84.5 2.4 select_maximum_fusion.2
  86.9 3.3 %slice_add_fusion.10 = f32[8,2,16,16,128]{4,3,2,0,1:T(8,128)S(1)} fusion(f32[8,2,18,18,130]{4,3,2,0,1:T(8,128)S(1)} %select_maximum_fusion.2), kind=kLoop, calls=%fused_computation.31 | loop fusion | flops 2621440 | bytes 14680064 | tf_op jit(solution)/shard_map/add | solution.py:17
  90.2 0.8 multiply_subtract_fusion.5
  91.0 2.4 select_maximum_fusion.1
  93.4 3.3 %slice_add_fusion.5 = f32[8,2,16,16,128]{4,3,2,0,1:T(8,128)S(1)} fusion(f32[8,2,18,18,130]{4,3,2,0,1:T(8,128)S(1)} %select_maximum_fusion.1), kind=kLoop, calls=%fused_computation.26 | loop fusion | flops 2621440 | bytes 14680064 | tf_op jit(solution)/shard_map/add | solution.py:17
  96.7 0.8 multiply_subtract_fusion.4
  97.4 2.4 select_maximum_fusion
  99.9 3.5 %slice_add_fusion = f32[8,2,16,16,128]{4,3,2,0,1:T(8,128)S(1)} fusion(f32[8,2,18,18,130]{4,3,2,0,1:T(8,128)S(1)} %select_maximum_fusion), kind=kLoop, calls=%fused_computation.21 | loop fusion | flops 2621440 | bytes 14680064 | tf_op jit(solution)/shard_map/add | solution.py:17
  103.4 0.9 multiply_subtract_fusion.1
  104.3 0.5 multiply_subtract_fusion
  104.8 0.4 maximum_bitcast_fusion
  105.2 0.4 pad_maximum_fusion
  105.7 0.6 copy.17
  106.3 51.6 %all_to_all.36 = f32[2,2,8,16,16,128]{5,4,2,1,0,3:T(8,128)S(1)} all-to-all(f32[2,2,8,16,16,128]{5,4,2,1,0,3:T(8,128)S(1)} %copy.17), channel_id=1, replica_groups=mesh['node'=4,'dom'=8] {'dom'}, dimensions={3} | all-to-all | bytes 8388608 | tf_op jit(solution)/shard_map/all_to_all | solution.py:84
  157.9 0.5 copy.19
  158.4 0.0 copy-start.1
  158.4 0.5 bitcast_reduce_fusion
  159.0 0.5 copy-done.1
  159.5 3.1 %fusion.10 = f32[2,2,32,32]{3,2,1,0:T(8,128)S(1)} fusion(f32[2,2,32,2,16,128]{5,4,3,2,1,0:T(8,128)S(1)} %bitcast_reduce_fusion, f32[32,2,16,128,1,1]{3,2,1,0,5,4:T(8,128)S(1)} %bitcast.53), kind=kOutput, calls=%fused_computation.66 | convolution fusion | flops 201330688 | bytes 2637824 | tf_op jit(solution)/shard_map/dot_general | solution.py:88
  162.6 0.0 all-reduce.10.cloned.1.call-start
  162.6 0.7 all-reduce.10.cloned.1.call-update
  163.3 23.5 %psum.22 = f32[2,2,32,32]{3,2,1,0:T(8,128)S(1)} all-reduce(f32[2,2,32,32]{3,2,1,0:T(8,128)S(1)} %fusion.10), channel_id=1, replica_groups=mesh['node'=4,'dom'=8] {'dom'}, use_global_device_ids=true, to_apply=%region_2.3 | all-reduce | flops 4096 | bytes 32768 | tf_op jit(solution)/shard_map/psum | solution.py:97
  186.8 23.4 %psum.23 = f32[2,2,32,32]{3,2,1,0:T(8,128)} all-reduce(f32[2,2,32,32]{3,2,1,0:T(8,128)S(1)} %psum.22), channel_id=1, replica_groups=mesh['node'=4,'dom'=8] {'node'}, use_global_device_ids=true, to_apply=%region_3.4 | all-reduce | flops 4096 | bytes 32768 | tf_op jit(solution)/shard_map/psum | solution.py:96
  210.2 43.2 %all-reduce.10.cloned.1.call-done = f32[2,2,32,2,16,128]{5,4,3,2,1,0:T(8,128)} async-done(((f32[2,2,32,2,16,128]{5,4,3,2,1,0:T(8,128)}), f32[2,2,32,2,16,128]{5,4,3,2,1,0:T(8,128)}) %all-reduce.10.cloned.1.call-update) | async-done | bytes 2097168 | tf_op jit(solution)/shard_map/psum | solution.py:99
  253.4 1.9 constant_dynamic-slice_fusion
  (10 shorter events, 0.1 us)
Async XLA Ops:
  7.2 7.4 %copy-start.2 = (f32[2,16,128]{2,1,0:T(8,128)S(1)}, f32[2,16,128]{2,1,0:T(8,128)}, u32[]{:S(2)}) copy-start(f32[2,16,128]{2,1,0:T(8,128)} %param.5) | copy-start | bytes 49156
  7.2 26.2 %copy-start.3 = (f32[2,16,128]{2,1,0:T(8,128)S(1)}, f32[2,16,128]{2,1,0:T(8,128)}, u32[]{:S(2)}) copy-start(f32[2,16,128]{2,1,0:T(8,128)} %param.6) | copy-start | bytes 49156
  7.2 34.5 %copy-start.4 = (f32[2,16,128]{2,1,0:T(8,128)S(1)}, f32[2,16,128]{2,1,0:T(8,128)}, u32[]{:S(2)}) copy-start(f32[2,16,128]{2,1,0:T(8,128)} %param.7) | copy-start | bytes 49156
  9.4 41.5 %all-to-all-start = ((f32[64,2,16,128]{3,2,1,0:T(8,128)}), f32[64,2,16,128]{3,2,1,0:T(8,128)S(1)}, u32[]{:S(2)}, u32[]{:S(2)}) async-start(f32[64,2,16,128]{3,2,1,0:T(8,128)} %bitcast), calls=%async_computation | async-start | bytes 2097152 | tf_op jit(solution)/shard_map/all_to_all | solution.py:58
  158.4 1.0 copy-start.1
  159.0 3.6 %copy-start = (f32[2,2,32,2,16,128]{5,4,3,2,1,0:T(8,128)}, f32[2,2,32,2,16,128]{5,4,3,2,1,0:T(8,128)S(1)}, u32[]{:S(2)}) copy-start(f32[2,2,32,2,16,128]{5,4,3,2,1,0:T(8,128)S(1)} %bitcast_reduce_fusion) | copy-start | bytes 6291460
  162.6 90.8 %all-reduce.10.cloned.1.call-start = ((), (), s32[]{:S(2)}) async-start(), calls=%async_computation.2 | async-start | bytes 4194304 | tf_op jit(solution)/shard_map/psum | solution.py:99
Sparse Core Ops, SparseCore 0:
  165.7 87.5 all-reduce.9
